TPU v7x, 32 devices: a whole 2x2x4 slice. The times are simulated.
32 devices in a mesh: shard: 4 (over y, x), ctx: 2 (over core), tp: 4 (over z).
Axes of the slice: x: 2, y: 2, z: 4, core: 2. Of those that a mesh axis runs over, the one named last changes fastest.
Arguments:
- tokens: bfloat16 [4, 1024, 1536], P('shard', ('ctx', 'tp')), may hold values from -6 to 6
- cotangent: bfloat16 [4, 1024, 1536], P('shard', ('ctx', 'tp')), may hold values from -6 to 6
- lengths: int32 [4], P('shard'), may hold values from 256 to 1024, as said below
- w_qkv: bfloat16 [1536, 3, 1536], P(('shard', 'ctx'), None, 'tp'), may hold values from -0.15625 to 0.15625
- w_forget: bfloat16 [1536, 24], P(('shard', 'ctx'), 'tp'), may hold values from -0.15625 to 0.15625
- forget_bias: float32 [24], replicated, may hold values from 3 to 8
- w_ogate: bfloat16 [1536, 1536], P(('shard', 'ctx'), 'tp'), may hold values from -0.15625 to 0.15625
- w_out: bfloat16 [1536, 1536], P(('shard', 'ctx'), 'tp'), may hold values from -0.625 to 0.625
- w_gu: bfloat16 [1536, 2, 4096], P(('shard', 'ctx'), None, 'tp'), may hold values from -0.15625 to 0.15625
- w_down: bfloat16 [1536, 4096], P(('shard', 'ctx'), 'tp'), may hold values from -0.09375 to 0.09375
- gain_attn: float32 [1536], replicated, may hold values from 0.5 to 1.5
- gain_mlp: float32 [1536], replicated, may hold values from 0.5 to 1.5
- qk_gain: float32 [2, 64], replicated, may hold values from 1 to 2
Outputs:
- output: bfloat16 [4, 1024, 1536], P('shard', ('ctx', 'tp'))
- input_grad: bfloat16 [4, 1024, 1536], P('shard', ('ctx', 'tp'))
- grad_qkv: float32 [1536, 3, 1536], P(('shard', 'ctx'), None, 'tp')
- grad_forget: float32 [1536, 24], P(('shard', 'ctx'), 'tp')
- grad_forget_bias: float32 [24], replicated
- grad_ogate: float32 [1536, 1536], P(('shard', 'ctx'), 'tp')
- grad_out: float32 [1536, 1536], P(('shard', 'ctx'), 'tp')
- grad_gu: float32 [1536, 2, 4096], P(('shard', 'ctx'), None, 'tp')
- grad_down: float32 [1536, 4096], P(('shard', 'ctx'), 'tp')
- grad_gain_attn: float32 [1536], replicated
- grad_gain_mlp: float32 [1536], replicated
- grad_qk_gain: float32 [2, 64], replicated
Inputs may be any that keep to these rules, and one draw needn't show every extreme that they name: `lengths`: real tokens of a slot; positions at or past it are padding; both the least and the most value occur in every draw.
All inputs are finite; a program needn't handle non-finite values.
Results may differ from a plain program's by a relative error of at most 0.04.
Values may be sent and summed in bfloat16 or wider, within the bound.
No kernel may reach another device: no remote copies, remote signals or barrier semaphores. Data moves between devices by JAX's collectives and lax.ppermute only.
A program may use at most 128 MiB of HBM per device.

v0:
```python
import math
import jax
import jax.numpy as jnp
from jax import lax
from jax.sharding import PartitionSpec as P

epsilon = 1e-06


def shifted(block, axis, distance):
    devices = range(lax.axis_size(axis))
    route = [(i - distance, i) for i in devices if i - distance in devices]
    return lax.ppermute(block, axis, route)


def norm_rows(values, gain):
    return values * lax.rsqrt(jnp.mean(values * values, axis=-1, keepdims=True) + epsilon) * gain


def product(left, right):
    return jnp.dot(left, right, preferred_element_type=jnp.float32)


def product_t(left, right):
    return lax.dot_general(
        left, right, (((1,), (1,)), ((), ())), preferred_element_type=jnp.float32
    )


def outer_rows(left, right):
    return lax.dot_general(
        left, right, (((0,), (0,)), ((), ())), preferred_element_type=jnp.float32
    )


def body(
    tokens,
    cotangent,
    lengths,
    w_qkv,
    w_forget,
    forget_bias,
    w_ogate,
    w_out,
    w_gu,
    w_down,
    gain_attn,
    gain_mlp,
    qk_gain,
):
    slot_count, own_rows, model_width = tokens.shape
    tensor_size = lax.axis_size("tp")
    tensor_place = lax.axis_index("tp")
    span_index = lax.axis_index("ctx")
    half_rows = own_rows * tensor_size
    row_count = slot_count * half_rows
    local_heads = w_forget.shape[1]
    head_size = qk_gain.shape[1]
    head_cols = local_heads * head_size
    hidden_units = w_down.shape[1]
    item_count = slot_count * local_heads
    score_scale = 1.0 / math.sqrt(head_size)
    own_start = tensor_place * own_rows
    full_tokens, full_cot = (
        lax.all_gather(tokens, "tp", axis=1, tiled=True),
        lax.all_gather(cotangent, "tp", axis=1, tiled=True),
    )
    qkv_full, forget_full, ogate_full, out_full, gu_full, down_full = (
        lax.all_gather(w_qkv, ("shard", "ctx"), axis=0, tiled=True),
        lax.all_gather(w_forget, ("shard", "ctx"), axis=0, tiled=True),
        lax.all_gather(w_ogate, ("shard", "ctx"), axis=0, tiled=True),
        lax.all_gather(w_out, ("shard", "ctx"), axis=0, tiled=True),
        lax.all_gather(w_gu, ("shard", "ctx"), axis=0, tiled=True),
        lax.all_gather(w_down, ("shard", "ctx"), axis=0, tiled=True),
    )
    qkv_flat = qkv_full.reshape(model_width, 3 * head_cols)
    gu_flat = gu_full.reshape(model_width, 2 * hidden_units)

    def own_slice(values):
        return lax.dynamic_slice_in_dim(
            values.reshape(slot_count, half_rows, values.shape[-1]), own_start, own_rows, 1
        )

    positions = span_index * half_rows + jnp.arange(half_rows, dtype=jnp.int32)
    valid_rows = (positions[None, :] < lengths[:, None]).astype(jnp.float32).reshape(row_count, 1)
    own_positions = span_index * half_rows + own_start + jnp.arange(own_rows, dtype=jnp.int32)
    valid_own = (own_positions[None, :] < lengths[:, None]).astype(jnp.float32)[:, :, None]
    residual = full_tokens.reshape(row_count, model_width).astype(jnp.float32)
    normed = norm_rows(residual, gain_attn).astype(jnp.bfloat16)
    qkv_rows = product(normed, qkv_flat).reshape(row_count, 3, head_cols)
    query_raw = qkv_rows[:, 0].reshape(row_count, local_heads, head_size)
    key_raw = qkv_rows[:, 1].reshape(row_count, local_heads, head_size)
    queries = (
        norm_rows(query_raw, qk_gain[0])
        .astype(jnp.bfloat16)
        .reshape(slot_count, half_rows, head_cols)
    )
    keys_here = (
        norm_rows(key_raw, qk_gain[1])
        .astype(jnp.bfloat16)
        .reshape(slot_count, half_rows, head_cols)
    )
    values_here = qkv_rows[:, 2].astype(jnp.bfloat16).reshape(slot_count, half_rows, head_cols)
    bias_here = lax.dynamic_slice_in_dim(forget_bias, tensor_place * local_heads, local_heads)
    forget_pre = (product(normed, forget_full) + bias_here).reshape(
        slot_count, half_rows, local_heads
    )
    cum_here = jnp.cumsum(jax.nn.log_sigmoid(forget_pre), axis=1)
    keys_left, values_left = shifted((keys_here, values_here), "ctx", 1)
    cum_left = shifted(cum_here, "ctx", 1)
    cum_query = cum_here + cum_left[:, -1:, :]

    def by_head(values):
        shaped = values.reshape(slot_count, half_rows, local_heads, head_size)
        return jnp.transpose(shaped, (0, 2, 1, 3)).reshape(item_count, half_rows, head_size)

    def by_head_cum(values):
        return jnp.transpose(values, (0, 2, 1)).reshape(item_count, half_rows)

    def to_slots(values):
        shaped = values.reshape(slot_count, local_heads, half_rows, head_size)
        return jnp.transpose(shaped, (0, 2, 1, 3)).reshape(slot_count, half_rows, head_cols)

    def to_slots_cum(values):
        return jnp.transpose(values.reshape(slot_count, local_heads, half_rows), (0, 2, 1))

    q_items = by_head(queries)
    k_items = jnp.concatenate([by_head(keys_left), by_head(keys_here)], axis=1)
    v_items = jnp.concatenate([by_head(values_left), by_head(values_here)], axis=1)
    cq_items = by_head_cum(cum_query)
    ck_items = jnp.concatenate([by_head_cum(cum_left), cq_items], axis=1)
    place_ids = jnp.arange(half_rows, dtype=jnp.int32)
    earlier = jnp.broadcast_to(span_index > 0, (half_rows, half_rows))
    allowed = jnp.concatenate([earlier, place_ids[None, :] <= place_ids[:, None]], axis=1)

    def score_block(query_block, key_block, cum_rows, cum_cols):
        score_raw = (
            product_t(query_block, key_block) * score_scale + cum_rows[:, None] - cum_cols[None, :]
        )
        return jnp.where(allowed, score_raw, -jnp.inf)

    def forward_item(pieces):
        query_block, key_block, value_block, cum_rows, cum_cols = pieces
        score_vals = score_block(query_block, key_block, cum_rows, cum_cols)
        row_max = jnp.max(score_vals, axis=1, keepdims=True)
        expo = jnp.exp(score_vals - row_max)
        row_total = jnp.sum(expo, axis=1, keepdims=True)
        attn_probs = (expo / row_total).astype(jnp.bfloat16)
        return (product(attn_probs, value_block), (row_max + jnp.log(row_total))[:, 0])

    attended_items, lse_items = lax.map(
        forward_item, (q_items, k_items, v_items, cq_items, ck_items)
    )
    attended_rows = to_slots(attended_items).reshape(row_count, head_cols)
    opener = jax.nn.sigmoid(product(normed, ogate_full))
    gated = (attended_rows * opener).astype(jnp.bfloat16)
    branch_part = product_t(gated, out_full)
    branch_full = lax.psum(branch_part, "tp")
    middle = residual + branch_full
    middle_share = own_slice(middle)
    normed_mid = norm_rows(middle, gain_mlp).astype(jnp.bfloat16)
    both = product(normed_mid, gu_flat).reshape(row_count, 2, hidden_units)
    gate_pre = both[:, 0]
    up_pre = both[:, 1]
    gate_sig = jax.nn.sigmoid(gate_pre)
    hidden = (gate_pre * gate_sig * up_pre).astype(jnp.bfloat16)
    down_share = lax.psum_scatter(
        product_t(hidden, down_full)
        .reshape(slot_count, half_rows, model_width)
        .astype(jnp.bfloat16),
        "tp",
        scatter_dimension=1,
        tiled=True,
    ).astype(jnp.float32)
    output = (valid_own * (middle_share + down_share)).astype(jnp.bfloat16)
    cot_rows = full_cot.reshape(row_count, model_width) * valid_rows.astype(jnp.bfloat16)
    d_hidden = product(cot_rows, down_full)
    d_gate = d_hidden * up_pre * gate_sig * (1.0 + gate_pre * (1.0 - gate_sig))
    d_up = d_hidden * gate_pre * gate_sig
    d_both = (
        jnp.stack([d_gate, d_up], axis=1).astype(jnp.bfloat16).reshape(row_count, 2 * hidden_units)
    )
    grad_down = outer_rows(cot_rows, hidden)
    grad_gu = outer_rows(normed_mid, d_both).reshape(model_width, 2, hidden_units)
    d_mid_terms = product_t(d_both, gu_flat)
    d_normed_mid = lax.psum(d_mid_terms, "tp")
    _, pull_mid = jax.vjp(norm_rows, middle, gain_mlp)
    d_middle_norm, d_gain_mlp_all = pull_mid(d_normed_mid)
    d_middle = d_middle_norm + cot_rows.astype(jnp.float32)
    feat_share = model_width // tensor_size
    owner = jnp.arange(model_width, dtype=jnp.int32) // feat_share == tensor_place
    d_gain_mlp_own = jnp.where(owner, d_gain_mlp_all, 0.0)
    d_branch = d_middle.astype(jnp.bfloat16)
    d_middle_share = own_slice(d_middle)
    d_gated = product(d_branch, out_full)
    grad_out = outer_rows(d_branch, gated)
    d_attended = (d_gated * opener).astype(jnp.bfloat16)
    d_open = (d_gated * attended_rows * opener * (1.0 - opener)).astype(jnp.bfloat16)
    grad_ogate = outer_rows(normed, d_open)
    da_items = by_head(d_attended.reshape(slot_count, half_rows, head_cols))

    def backward_item(pieces):
        query_block, key_block, value_block, cum_rows, cum_cols, lse_block, grad_block = pieces
        score_vals = score_block(query_block, key_block, cum_rows, cum_cols)
        attn_probs = jnp.exp(score_vals - lse_block[:, None])
        d_probs = product_t(grad_block, value_block)
        centre = jnp.sum(attn_probs * d_probs, axis=1, keepdims=True)
        d_scores = (attn_probs * (d_probs - centre)).astype(jnp.bfloat16)
        d_query_block = product(d_scores, key_block) * score_scale
        d_key_block = outer_rows(d_scores, query_block) * score_scale
        d_value_block = outer_rows(attn_probs.astype(jnp.bfloat16), grad_block)
        d_cum_rows = jnp.sum(d_scores, axis=1, dtype=jnp.float32)
        d_cum_cols = -jnp.sum(d_scores, axis=0, dtype=jnp.float32)
        return (d_query_block, d_key_block, d_value_block, d_cum_rows, d_cum_cols)

    dq_items, dk_items, dv_items, dcq_items, dck_items = lax.map(
        backward_item, (q_items, k_items, v_items, cq_items, ck_items, lse_items, da_items)
    )
    dc_own = dcq_items + dck_items[:, half_rows:]
    dc_left = dck_items[:, :half_rows]
    dc_left = dc_left.at[:, -1].add(jnp.sum(dc_own, axis=1))
    back_keys, back_values, back_cum = (
        shifted(to_slots(dk_items[:, :half_rows]).astype(jnp.bfloat16), "ctx", -1).astype(
            jnp.float32
        ),
        shifted(to_slots(dv_items[:, :half_rows]).astype(jnp.bfloat16), "ctx", -1).astype(
            jnp.float32
        ),
        shifted(to_slots_cum(dc_left).astype(jnp.bfloat16), "ctx", -1).astype(jnp.float32),
    )
    d_query = to_slots(dq_items).reshape(row_count, local_heads, head_size)
    d_key = (to_slots(dk_items[:, half_rows:]) + back_keys).reshape(
        row_count, local_heads, head_size
    )
    d_value = (to_slots(dv_items[:, half_rows:]) + back_values).reshape(row_count, head_cols)
    d_cum = to_slots_cum(dc_own) + back_cum
    d_log = jnp.flip(jnp.cumsum(jnp.flip(d_cum, 1), axis=1), 1)
    d_forget = d_log * jax.nn.sigmoid(-forget_pre)
    d_bias_own = jnp.sum(d_forget, axis=(0, 1))
    d_forget_low = d_forget.reshape(row_count, local_heads).astype(jnp.bfloat16)
    grad_forget = outer_rows(normed, d_forget_low)
    _, pull_query = jax.vjp(norm_rows, query_raw, qk_gain[0])
    d_query_raw, d_query_gain = pull_query(d_query)
    _, pull_key = jax.vjp(norm_rows, key_raw, qk_gain[1])
    d_key_raw, d_key_gain = pull_key(d_key)
    d_mixed = (
        jnp.stack(
            [
                d_query_raw.reshape(row_count, head_cols),
                d_key_raw.reshape(row_count, head_cols),
                d_value,
            ],
            axis=1,
        )
        .astype(jnp.bfloat16)
        .reshape(row_count, 3 * head_cols)
    )
    grad_qkv = outer_rows(normed, d_mixed).reshape(model_width, 3, head_cols)
    d_normed = (
        product_t(d_mixed, qkv_flat)
        + product_t(d_open, ogate_full)
        + product_t(d_forget_low, forget_full)
    )
    root = lax.rsqrt(jnp.mean(residual * residual, axis=1, keepdims=True) + epsilon)
    unit = residual * root
    d_unit = d_normed * gain_attn
    dot_part = (jnp.sum(d_unit * unit, axis=1) / model_width).reshape(slot_count, half_rows)
    d_unit_share, dot_full = (
        lax.psum_scatter(
            d_unit.reshape(slot_count, half_rows, model_width).astype(jnp.bfloat16),
            "tp",
            scatter_dimension=1,
            tiled=True,
        ).astype(jnp.float32),
        lax.psum_scatter(
            dot_part.astype(jnp.bfloat16), "tp", scatter_dimension=1, tiled=True
        ).astype(jnp.float32),
    )
    unit_share = own_slice(unit)
    root_share = own_slice(root)
    input_grad = (
        d_middle_share + root_share * (d_unit_share - unit_share * dot_full[:, :, None])
    ).astype(jnp.bfloat16)
    grad_parts = (
        lax.psum_scatter(
            grad_qkv.astype(jnp.bfloat16), ("shard", "ctx"), scatter_dimension=0, tiled=True
        ).astype(jnp.float32),
        lax.psum_scatter(
            grad_forget.astype(jnp.bfloat16), ("shard", "ctx"), scatter_dimension=0, tiled=True
        ).astype(jnp.float32),
        lax.psum_scatter(
            grad_ogate.astype(jnp.bfloat16), ("shard", "ctx"), scatter_dimension=0, tiled=True
        ).astype(jnp.float32),
        lax.psum_scatter(
            grad_out.astype(jnp.bfloat16), ("shard", "ctx"), scatter_dimension=0, tiled=True
        ).astype(jnp.float32),
        lax.psum_scatter(
            grad_gu.astype(jnp.bfloat16), ("shard", "ctx"), scatter_dimension=0, tiled=True
        ).astype(jnp.float32),
        lax.psum_scatter(
            grad_down.astype(jnp.bfloat16), ("shard", "ctx"), scatter_dimension=0, tiled=True
        ).astype(jnp.float32),
    )
    bias_full = lax.dynamic_update_slice_in_dim(
        jnp.zeros(forget_bias.shape, jnp.float32), d_bias_own, tensor_place * local_heads, 0
    )
    gain_attn_part = jnp.sum(d_normed * unit, axis=0)
    small_parts = lax.psum(
        (gain_attn_part, d_gain_mlp_own, jnp.stack([d_query_gain, d_key_gain]), bias_full),
        ("shard", "ctx", "tp"),
    )
    return (
        output,
        input_grad,
        grad_parts[0],
        grad_parts[1],
        small_parts[3],
        grad_parts[2],
        grad_parts[3],
        grad_parts[4],
        grad_parts[5],
        small_parts[0],
        small_parts[1],
        small_parts[2],
    )


def solution(mesh):
    return jax.shard_map(
        body,
        mesh=mesh,
        in_specs=(
            P("shard", ("ctx", "tp"), None),
            P("shard", ("ctx", "tp"), None),
            P("shard"),
            P(("shard", "ctx"), None, "tp"),
            P(("shard", "ctx"), "tp"),
            P(),
            P(("shard", "ctx"), "tp"),
            P(("shard", "ctx"), "tp"),
            P(("shard", "ctx"), None, "tp"),
            P(("shard", "ctx"), "tp"),
            P(),
            P(),
            P(),
        ),
        out_specs=(
            P("shard", ("ctx", "tp"), None),
            P("shard", ("ctx", "tp"), None),
            P(("shard", "ctx"), None, "tp"),
            P(("shard", "ctx"), "tp"),
            P(),
            P(("shard", "ctx"), "tp"),
            P(("shard", "ctx"), "tp"),
            P(("shard", "ctx"), None, "tp"),
            P(("shard", "ctx"), "tp"),
            P(),
            P(),
            P(),
        ),
        check_vma=False,
    )
```

profile of v0, /device:TPU:0, one launch (start us, length us, event | category | flops | bytes accessed | tf_op | source)
XLA Modules:
  0.0 1049.7 jit_solution(11627350117377922482)
XLA Ops:
  11.9 10.6 %all-gather = bf16[8,192,6]{1,2,0:T(8,128)(2,1)S(1)} all-gather(bf16[1,192,6]{1,2,0:T(8,128)(2,1)} %bitcast.510), channel_id=1, replica_groups=mesh['shard'=4,'ctx'=2,'tp'=4] {'shard','ctx'}, dimensions={0}, use_global_device_ids=true | all-gather | bytes 20736 | tf_op jit(solution)/shard_map/all_gather | solution.py:70
  24.6 24.8 %all-gather.9.cloned.1.call-done = bf16[1,512,1536]{2,1,0:T(8,128)(2,1)} async-done(((bf16[1,128,1536]{2,1,0:T(8,128)(2,1)}), bf16[1,512,1536]{2,1,0:T(8,128)(2,1)}) %all-gather.9.cloned.1.call-update) | async-done | bytes 1572880 | tf_op jit(solution)/shard_map/all_gather | solution.py:65
  59.5 24.7 %all-gather.11.cloned.1.call-done = bf16[1536,3,384]{2,0,1:T(8,128)(2,1)} async-done(((bf16[192,3,384]{2,0,1:T(8,128)(2,1)}), bf16[1536,3,384]{2,0,1:T(8,128)(2,1)}) %all-gather.11.cloned.1.call-update) | async-done | bytes 3538960 | tf_op jit(solution)/shard_map/all_gather | solution.py:69
  84.2 6.1 copy.92
  90.3 4.1 fusion.41
  96.7 2.9 collective-permute-start
  106.8 3.3 fusion.74
  110.1 2.2 copy.94
  112.2 2.2 copy.101
  118.7 37.0 %while.31 = (s32[]{:T(128)}, f32[6,512,64]{1,2,0:T(8,128)}, f32[6,512]{1,0:T(8,128)S(1)}, bf16[6,512,64]{2,1,0:T(8,128)(2,1)}, bf16[6,1024,64]{2,1,0:T(8,128)(2,...) while((s32[]{:T(128)}, f32[6,512,64]{1,2,0:T(8,128)}, ...), condition=%wide.region_8.9_spmd, body=%wide.region_5.8_spmd.sunk | while | flops 139460096 | bytes 7643265 | solution.py:151
  122.5 2.2 fusion.162
  128.7 2.3 fusion.162
  134.9 2.2 fusion.162
  141.0 2.2 fusion.162
  147.2 2.2 fusion.162
  153.3 2.2 fusion.162
  156.2 3.4 fusion.84
  159.7 4.0 fusion.126
  168.9 116.0 %all-reduce.5.cloned.1.call-done = f32[512,1536]{1,0:T(8,128)} async-done(((f32[512,1536]{1,0:T(8,128)}), f32[512,1536]{1,0:T(8,128)}) %all-reduce.5.cloned.1.call-update) | async-done | bytes 3145744 | tf_op jit(solution)/shard_map/psum | solution.py:158
  284.9 2.8 multiply_reduce_fusion.5
  289.3 42.5 %all-gather.17.cloned.1.call-done = bf16[1536,2,1024]{2,0,1:T(8,128)(2,1)} async-done(((bf16[192,2,1024]{2,0,1:T(8,128)(2,1)}), bf16[1536,2,1024]{2,0,1:T(8,128)(2,1)}) %all-gather.17.cloned.1.call-update) | async-done | bytes 6291472 | tf_op jit(solution)/shard_map/all_gather | solution.py:73
  331.8 8.7 copy.104
  340.5 8.1 fusion.36
  348.6 21.9 %all-gather.21.cloned.1.call-done = bf16[1,512,1536]{2,1,0:T(8,128)(2,1)} async-done(((bf16[1,128,1536]{2,1,0:T(8,128)(2,1)}), bf16[1,512,1536]{2,1,0:T(8,128)(2,1)}) %all-gather.21.cloned.1.call-update) | async-done | bytes 1572880 | tf_op jit(solution)/shard_map/all_gather | solution.py:66
  370.5 33.1 %all-gather.19.cloned.1.call-done = bf16[1536,1024]{1,0:T(8,128)(2,1)} async-done(((bf16[192,1024]{1,0:T(8,128)(2,1)}), bf16[1536,1024]{1,0:T(8,128)(2,1)}) %all-gather.19.cloned.1.call-update) | async-done | bytes 3145744 | tf_op jit(solution)/shard_map/all_gather | solution.py:74
  403.6 5.9 fusion.52
  410.9 8.0 convolution_bitcast_fusion.2
  423.5 6.7 fusion.47
  430.5 109.7 %all-reduce.7.cloned.1.call-done = f32[512,1536]{1,0:T(8,128)} async-done(((f32[512,1536]{1,0:T(8,128)}), f32[512,1536]{1,0:T(8,128)}) %all-reduce.7.cloned.1.call-update) | async-done | bytes 3145744 | tf_op jit(solution)/shard_map/psum | solution.py:186
  540.2 3.4 multiply_reduce_fusion.1
  543.7 3.0 fusion.46
  548.5 2.2 copy.105
  552.2 97.2 %while.32 = (s32[]{:T(128)}, f32[6,512,64]{1,2,0:T(8,128)}, f32[6,1024,64]{1,2,0:T(8,128)}, f32[6,1024,64]{1,2,0:T(8,128)}, f32[6,512]{1,0:T(8,128)}, /*index=5*...) while((s32[]{:T(128)}, f32[6,512,64]{1,2,0:T(8,128)}, ...), condition=%wide.region_18.19_spmd, body=%wide.region_14.18_spmd.sunk | while | flops 342981632 | bytes 20376776 | solution.py:216
  555.3 2.1 multiply_reduce_fusion.11
  571.5 2.1 multiply_reduce_fusion.11
  587.6 2.1 multiply_reduce_fusion.11
  603.8 2.1 multiply_reduce_fusion.11
  620.1 2.1 multiply_reduce_fusion.11
  636.2 2.1 multiply_reduce_fusion.11
  651.3 2.1 slice.88
  667.2 2.3 fusion.80
  672.4 2.7 rev.7
  676.4 4.1 reduce-window.16
  691.2 2.7 rev.8
  695.9 2.6 convolution_convert_fusion.6
  700.6 2.3 multiply_reduce_fusion.6
  707.6 2.3 convolution_bitcast_fusion.3
  711.4 3.4 multiply_reduce_fusion.2
  715.7 6.4 convolution_convert_fusion.2
  722.2 3.7 convolution_convert_fusion.5
  729.0 5.8 convolution_convert_fusion.1
  734.9 3.1 maximum_convert_fusion
  738.0 4.0 copy.114
  742.0 8.9 convolution_convert_fusion
  751.6 2.1 fusion.89
  755.5 41.1 %all-reduce.1 = (f32[24]{0:T(128)}, f32[1536]{0:T(1024)}, f32[1536]{0:T(1024)}, f32[2,64]{1,0:T(2,128)}) all-reduce(f32[24]{0:T(128)S(1)} %dynamic_update_slice.28, f32[1536]{0:T(1024)S(1)} %get-tuple-element.207, f32[1536]{0:T(1024)S(1)} %fusion.108, ...), channel_id=1, replica_groups=mesh['shard'=4,'ctx'=2,'tp'=4] {'shard','ctx','tp'}, use_global_device_ids=true, to_apply=%region_30.31 | all-reduce | flops 3224 | bytes 25792 | tf_op jit(solution)/shard_map/psum | solution.py:308
  797.5 8.2 reduce-scatter.26.cloned.1.call-done
  807.7 37.9 %reduce-scatter.20.cloned.1.call-done = bf16[192,384]{1,0:T(8,128)(2,1)} async-done(((bf16[1536,384]{1,0:T(8,128)(2,1)}), bf16[192,384]{1,0:T(8,128)(2,1)}) %reduce-scatter.20.cloned.1.call-update) | async-done | bytes 147472 | tf_op jit(solution)/shard_map/reduce_scatter | solution.py:291
  847.2 38.6 %reduce-scatter.22.cloned.1.call-done = bf16[192,384]{1,0:T(8,128)(2,1)} async-done(((bf16[1536,384]{1,0:T(8,128)(2,1)}), bf16[192,384]{1,0:T(8,128)(2,1)}) %reduce-scatter.22.cloned.1.call-update) | async-done | bytes 147472 | tf_op jit(solution)/shard_map/reduce_scatter | solution.py:294
  887.5 36.4 %reduce-scatter.16.cloned.1.call-done = bf16[1,128,1536]{2,1,0:T(8,128)(2,1)} async-done(((bf16[1,512,1536]{2,1,0:T(8,128)(2,1)}), bf16[1,128,1536]{2,1,0:T(8,128)(2,1)}) %reduce-scatter.16.cloned.1.call-update) | async-done | bytes 393232 | tf_op jit(solution)/shard_map/reduce_scatter | solution.py:269
  923.9 2.2 fusion.83
  926.1 48.2 %reduce-scatter.18.cloned.1.call-done = bf16[192,3,384]{2,0,1:T(8,128)(2,1)} async-done(((bf16[1536,3,384]{2,0,1:T(8,128)(2,1)}), bf16[192,3,384]{2,0,1:T(8,128)(2,1)}) %reduce-scatter.18.cloned.1.call-update) | async-done | bytes 442384 | tf_op jit(solution)/shard_map/reduce_scatter | solution.py:285
  976.3 63.0 %reduce-scatter.24.cloned.1.call-done = bf16[192,2,1024]{2,0,1:T(8,128)(2,1)} async-done(((bf16[1536,2,1024]{2,0,1:T(8,128)(2,1)}), bf16[192,2,1024]{2,0,1:T(8,128)(2,1)}) %reduce-scatter.24.cloned.1.call-update) | async-done | bytes 786448 | tf_op jit(solution)/shard_map/reduce_scatter | solution.py:297
  1039.3 3.1 copy.116
  (403 shorter events, 209.6 us)
Async XLA Ops:
  7.2 17.4 %copy-start.69 = (f32[24]{0:T(128)S(1)}, f32[24]{0:T(128)}, u32[]{:S(2)}) copy-start(f32[24]{0:T(128)} %param.24) | copy-start | bytes 292
  7.2 42.2 %all-gather.9.cloned.1.call-start = ((), (), s32[]{:S(2)}) async-start(), calls=%async_computation.9 | async-start | bytes 1966080 | tf_op jit(solution)/shard_map/all_gather | solution.py:65
  7.9 76.3 %all-gather.11.cloned.1.call-start = ((), (), s32[]{:S(2)}) async-start(), calls=%async_computation.10 | async-start | bytes 3981312 | tf_op jit(solution)/shard_map/all_gather | solution.py:69
  8.7 42.5 %copy-start.59 = (f32[1536]{0:T(1024)S(1)}, f32[1536]{0:T(1024)}, u32[]{:S(2)}) copy-start(f32[1536]{0:T(1024)} %param.29) | copy-start | bytes 18436
  8.7 147.0 %all-gather.13.cloned.1.call-start = ((), (), s32[]{:S(2)}) async-start(), calls=%async_computation.11 | async-start | bytes 1327104 | tf_op jit(solution)/shard_map/all_gather | solution.py:71
  9.4 150.3 %all-gather.15.cloned.1.call-start = ((), (), s32[]{:S(2)}) async-start(), calls=%async_computation.12 | async-start | bytes 1327104 | tf_op jit(solution)/shard_map/all_gather | solution.py:72
  10.0 274.9 %all-reduce.5.cloned.1.call-start = ((), (), s32[]{:S(2)}) async-start(), calls=%async_computation.13 | async-start | bytes 6291456 | tf_op jit(solution)/shard_map/psum | solution.py:158
  11.5 84.3 %copy-start.49 = (f32[384]{0:T(512)}, f32[384]{0:T(512)S(1)}, u32[]{:S(2)}) copy-start(f32[384]{0:T(512)S(1)} %mul.513) | copy-start | bytes 4612
  22.7 30.5 %copy-start.39 = (bf16[1536,6]{0,1:T(8,128)(2,1)}, bf16[1536,6]{0,1:T(8,128)(2,1)S(1)}, u32[]{:S(2)}) copy-start(bf16[1536,6]{0,1:T(8,128)(2,1)S(1)} %reshape.771) | copy-start | bytes 55300
  51.2 39.1 %copy-start.57 = (f32[512]{0:T(512)}, f32[512]{0:T(512)S(1)}, u32[]{:S(2)}) copy-start(f32[512]{0:T(512)S(1)} %add_rsqrt_fusion) | copy-start | bytes 6148
  53.2 5.0 copy-start.42
  55.5 2.4 collective-permute-start.1
  59.5 30.8 %copy-start.2 = (bf16[1,512,1536]{2,1,0:T(8,128)(2,1)S(1)}, bf16[1,512,1536]{2,1,0:T(8,128)(2,1)}, u32[]{:S(2)}) copy-start(bf16[1,512,1536]{2,1,0:T(8,128)(2,1)} %all-gather.9.cloned.1.call-done) | copy-start | bytes 4718596
  94.4 7.8 copy-start.4
  94.6 7.8 copy-start.9
  94.6 9.4 copy-start.6
  95.7 6.0 copy-start.37
  95.8 5.9 copy-start.35
  96.7 13.4 %collective-permute-start = (bf16[1,512,384]{1,2,0:T(8,128)(2,1)}, bf16[1,512,384]{1,2,0:T(8,128)(2,1)}, u32[]{:S(2)}, u32[]{:S(2)}) collective-permute-start(bf16[1,512,384]{1,2,0:T(8,128)(2,1)} %multiply_convert_fusion.9), channel_id=1, source_target_pairs={{0,4},{1,5},{2,6},{3,7},{8,12},{9,13},{10,14},{11,15},{16,20},{17,... | collective-permute-start | bytes 1179656 | tf_op jit(solution)/shard_map/ppermute | solution.py:13
  99.6 12.7 %collective-permute-start.2 = (bf16[1,512,384]{1,2,0:T(8,128)(2,1)}, bf16[1,512,384]{1,2,0:T(8,128)(2,1)}, u32[]{:S(2)}, u32[]{:S(2)}) collective-permute-start(bf16[1,512,384]{1,2,0:T(8,128)(2,1)} %slice_bitcast_fusion.5), channel_id=1, source_target_pairs={{0,4},{1,5},{2,6},{3,7},{8,12},{9,13},{10,14},{11,15},{16,20},{17,... | collective-permute-start | bytes 1179656 | tf_op jit(solution)/shard_map/ppermute | solution.py:13
  155.6 4.0 copy-start.10
  163.7 168.1 %all-gather.17.cloned.1.call-start = ((), (), s32[]{:S(2)}) async-start(), calls=%async_computation.14 | async-start | bytes 7077888 | tf_op jit(solution)/shard_map/all_gather | solution.py:73
  165.9 204.6 %all-gather.21.cloned.1.call-start = ((), (), s32[]{:S(2)}) async-start(), calls=%async_computation.17 | async-start | bytes 1966080 | tf_op jit(solution)/shard_map/all_gather | solution.py:66
  166.7 236.9 %all-gather.19.cloned.1.call-start = ((), (), s32[]{:S(2)}) async-start(), calls=%async_computation.15 | async-start | bytes 3538944 | tf_op jit(solution)/shard_map/all_gather | solution.py:74
  167.4 372.7 %all-reduce.7.cloned.1.call-start = ((), (), s32[]{:S(2)}) async-start(), calls=%async_computation.18 | async-start | bytes 6291456 | tf_op jit(solution)/shard_map/psum | solution.py:186
  287.8 252.4 %copy-start = (f32[512,1536]{1,0:T(8,128)}, f32[512,1536]{1,0:T(8,128)S(1)}, u32[]{:S(2)}) copy-start(f32[512,1536]{1,0:T(8,128)S(1)} %get-tuple-element.267) | copy-start | bytes 9437188
  418.9 332.6 %reduce-scatter.14.cloned.1.call-start = ((), (), s32[]{:S(2)}) async-start(), calls=%async_computation.16 | async-start | bytes 1966080 | tf_op jit(solution)/shard_map/reduce_scatter | solution.py:167
  430.2 323.7 %reduce-scatter.30.cloned.1.call-start = ((), (), s32[]{:S(2)}) async-start(), calls=%async_computation.26 | async-start | bytes 442368
  540.2 3.5 copy-start.54
  540.2 3.5 copy-start.8
  540.2 3.5 copy-start.19
  540.2 3.5 copy-start.44
  540.2 3.5 copy-start.51
  540.2 3.5 copy-start.65
  543.7 3.0 copy-start.12
  543.7 3.0 copy-start.16
  543.7 3.0 copy-start.25
  552.2 3.0 copy-start.1
  568.4 3.0 copy-start.1
  584.6 3.0 copy-start.1
  600.8 3.0 copy-start.1
  617.0 3.0 copy-start.1
  633.2 3.0 copy-start.1
  653.4 51.8 %collective-permute-start.4 = (bf16[1,512,384]{1,2,0:T(8,128)(2,1)}, bf16[1,512,384]{1,2,0:T(8,128)(2,1)}, u32[]{:S(2)}, u32[]{:S(2)}) collective-permute-start(bf16[1,512,384]{1,2,0:T(8,128)(2,1)} %bitcast.100), channel_id=1, source_target_pairs={{4,0},{5,1},{6,2},{7,3},{12,8},{13,9},{14,10},{15,11},{20,16},{21,... | collective-permute-start | bytes 1179656 | tf_op jit(solution)/shard_map/ppermute | solution.py:13
  656.6 44.0 %collective-permute-start.3 = (bf16[1,512,384]{1,2,0:T(8,128)(2,1)}, bf16[1,512,384]{1,2,0:T(8,128)(2,1)}, u32[]{:S(2)}, u32[]{:S(2)}) collective-permute-start(bf16[1,512,384]{1,2,0:T(8,128)(2,1)} %bitcast.90), channel_id=1, source_target_pairs={{4,0},{5,1},{6,2},{7,3},{12,8},{13,9},{14,10},{15,11},{20,16},{21,... | collective-permute-start | bytes 1179656 | tf_op jit(solution)/shard_map/ppermute | solution.py:13
  665.8 5.1 copy-start.24
  665.8 6.0 copy-start.34
  665.8 6.0 copy-start.38
  665.8 6.0 collective-permute-start.5
  700.3 96.4 %reduce-scatter.28.cloned.1.call-start = ((), (), s32[]{:S(2)}) async-start(), calls=%async_computation.25 | async-start | bytes 163840
  705.2 4.7 copy-start.27
  705.2 4.7 copy-start.29
  711.4 4.3 copy-start.66
  715.7 90.0 %reduce-scatter.26.cloned.1.call-start = ((), (), s32[]{:S(2)}) async-start(), calls=%async_computation.24 | async-start | bytes 3538944 | tf_op jit(solution)/shard_map/reduce_scatter | solution.py:300
  722.2 123.4 %reduce-scatter.20.cloned.1.call-start = ((), (), s32[]{:S(2)}) async-start(), calls=%async_computation.21 | async-start | bytes 1327104 | tf_op jit(solution)/shard_map/reduce_scatter | solution.py:291
  725.9 159.9 %reduce-scatter.22.cloned.1.call-start = ((), (), s32[]{:S(2)}) async-start(), calls=%async_computation.22 | async-start | bytes 1327104 | tf_op jit(solution)/shard_map/reduce_scatter | solution.py:294
  728.0 195.8 %reduce-scatter.16.cloned.1.call-start = ((), (), s32[]{:S(2)}) async-start(), calls=%async_computation.19 | async-start | bytes 1966080 | tf_op jit(solution)/shard_map/reduce_scatter | solution.py:269
  728.6 245.7 %reduce-scatter.18.cloned.1.call-start = ((), (), s32[]{:S(2)}) async-start(), calls=%async_computation.20 | async-start | bytes 3981312 | tf_op jit(solution)/shard_map/reduce_scatter | solution.py:285
  734.9 304.4 %reduce-scatter.24.cloned.1.call-start = ((), (), s32[]{:S(2)}) async-start(), calls=%async_computation.23 | async-start | bytes 7077888 | tf_op jit(solution)/shard_map/reduce_scatter | solution.py:297
  738.0 4.0 copy-start.45
  738.0 4.0 copy-start.52
  750.8 2.9 copy-start.68
  750.8 4.6 copy-start.56
  750.9 4.7 copy-start.67
  (35 other events, 59.1 us)
Sparse Core Ops, SparseCore 0:
  9.6 39.7 all-gather.8
  51.3 32.8 all-gather.10
  86.1 24.0 all-gather.12
  112.0 24.0 all-gather.14
  163.8 121.0 all-reduce.4
  287.2 44.5 all-gather.16
  333.4 37.0 all-gather.20
  372.4 31.1 all-gather.18
  419.0 121.0 all-reduce.6
  542.3 34.2 reduce-scatter.13
  700.4 35.1 reduce-scatter.29
  738.2 19.1 reduce-scatter.27
  761.2 44.4 reduce-scatter.25
  808.8 36.7 reduce-scatter.19
  849.0 36.7 reduce-scatter.21
  888.6 35.2 reduce-scatter.15
  927.2 47.0 reduce-scatter.17
  977.5 61.7 reduce-scatter.23
where the time goes:
time: 1060 us; the launch traced here: 1050 us
  waiting for transfers between devices  611 us (58%)
  matrix products  162 us (15%)
  local copies, waits for them, and re-layouts  121 us (11%)
  other arithmetic  75.4 us (7%)
  blocking collectives  51.8 us (5%)
  between operations  16.4 us (2%)
  starting transfers between devices  12.2 us (1%)
    psum x1, waiting for transfers between devices, body(): branch_full = lax.psum(branch_part, 'tp')  116 us
    psum x1, waiting for transfers between devices, body(): d_normed_mid = lax.psum(d_mid_terms, 'tp')  110 us
    reduce_scatter x1, waiting for transfers between devices, body(): lax.psum_scatter(grad_gu.astype(jnp.bfloat16), ('shard', 'ctx'), scatter_...  63 us
    dot_general x24, matrix products, product_t(): lax.dot_general(left, right, (((1,), (1,)), ((), ())), preferred_element_...  58 us
    dot_general x18, matrix products, outer_rows(): lax.dot_general(left, right, (((0,), (0,)), ((), ())), preferred_element_...  52.8 us
    dot_general x18, matrix products, product(): return jnp.dot(left, right, preferred_element_type=jnp.float32)  51.2 us
    reduce_scatter x1, waiting for transfers between devices, body(): lax.psum_scatter(grad_qkv.astype(jnp.bfloat16), ('shard', 'ctx'), scatter...  48.2 us
    all_gather x1, waiting for transfers between devices, body(): lax.all_gather(w_gu, ('shard', 'ctx'), axis=0, tiled=True)  42.5 us
  transfers between devices with their start and end apart: 24, of which 14 were waited for; matrix products, arithmetic and copies ran while one was open for 31% of the time, Pallas kernels for 0%

commit v1 on v0

--- a/solution.py
+++ b/solution.py
@@ -5,6 +5,18 @@
 from jax.sharding import PartitionSpec as P
 
 epsilon = 1e-06
+
+
+def gather_by_bits(x, axis, dim):
+    ways, here = (lax.axis_size(axis), lax.axis_index(axis))
+    grown, reach = (x, 1)
+    while reach < ways:
+        theirs = lax.ppermute(grown, axis, [(d, d ^ reach) for d in range(ways)])
+        mine_first = jnp.concatenate([grown, theirs], axis=dim)
+        theirs_first = jnp.concatenate([theirs, grown], axis=dim)
+        grown = jnp.where(here & reach == 0, mine_first, theirs_first)
+        reach = 2 * reach
+    return grown
 
 
 def shifted(block, axis, distance):
@@ -71,7 +83,7 @@
         lax.all_gather(w_ogate, ("shard", "ctx"), axis=0, tiled=True),
         lax.all_gather(w_out, ("shard", "ctx"), axis=0, tiled=True),
         lax.all_gather(w_gu, ("shard", "ctx"), axis=0, tiled=True),
-        lax.all_gather(w_down, ("shard", "ctx"), axis=0, tiled=True),
+        gather_by_bits(w_down, ("shard", "ctx"), 0),
     )
     qkv_flat = qkv_full.reshape(model_width, 3 * head_cols)
     gu_flat = gu_full.reshape(model_width, 2 * hidden_units)

time: 1060 us -> 1030 us (0.972)
  waiting for transfers between devices: 611 us -> 571 us
    all_gather x1 -> x0, waiting for transfers between devices: 33.1 us -> none  [body(): lax.all_gather(w_down, ('shard', 'ctx'), axis=0, tiled=True)]
    psum x1, waiting for transfers between devices: 116 us -> 93.3 us  [body(): branch_full = lax.psum(branch_part, 'tp')]
    ppermute x0 -> x3, waiting for transfers between devices: none -> 19.2 us  [gather_by_bits(): theirs = lax.ppermute(grown, axis, [(d, d ^ reach) for d in range(ways)])]
  transfers between devices with their start and end apart: 24 -> 26, of which waited for: 14 -> 15; matrix products, arithmetic and copies ran while one was open for 31% -> 33% of each run, Pallas kernels for 0% -> 0%
where the time goes in v1:
time: 1030 us; the launch traced here: 1020 us
  waiting for transfers between devices  571 us (55%)
  matrix products  164 us (16%)
  local copies, waits for them, and re-layouts  121 us (12%)
  other arithmetic  77.5 us (8%)
  blocking collectives  51.8 us (5%)
  between operations  15.8 us (2%)
  starting transfers between devices  15 us (1%)
    psum x1, waiting for transfers between devices, body(): d_normed_mid = lax.psum(d_mid_terms, 'tp')  108 us
    psum x1, waiting for transfers between devices, body(): branch_full = lax.psum(branch_part, 'tp')  93.3 us
    reduce_scatter x1, waiting for transfers between devices, body(): lax.psum_scatter(grad_gu.astype(jnp.bfloat16), ('shard', 'ctx'), scatter_...  63 us
    dot_general x24, matrix products, product_t(): lax.dot_general(left, right, (((1,), (1,)), ((), ())), preferred_element_...  58.6 us
    dot_general x18, matrix products, outer_rows(): lax.dot_general(left, right, (((0,), (0,)), ((), ())), preferred_element_...  52.9 us
    dot_general x18, matrix products, product(): return jnp.dot(left, right, preferred_element_type=jnp.float32)  52.5 us
    reduce_scatter x1, waiting for transfers between devices, body(): lax.psum_scatter(grad_qkv.astype(jnp.bfloat16), ('shard', 'ctx'), scatter...  48.2 us
    all_gather x1, waiting for transfers between devices, body(): lax.all_gather(w_gu, ('shard', 'ctx'), axis=0, tiled=True)  42.5 us
  transfers between devices with their start and end apart: 26, of which 15 were waited for; matrix products, arithmetic and copies ran while one was open for 33% of the time, Pallas kernels for 0%

profile of v1, /device:TPU:0, one launch (start us, length us, event | category | flops | bytes accessed | tf_op | source)
XLA Modules:
  0.0 1016.2 jit_solution(10547970498878797645)
XLA Ops:
  12.1 10.6 %all-gather = bf16[8,192,6]{1,2,0:T(8,128)(2,1)S(1)} all-gather(bf16[1,192,6]{1,2,0:T(8,128)(2,1)} %bitcast.508), channel_id=1, replica_groups=mesh['shard'=4,'ctx'=2,'tp'=4] {'shard','ctx'}, dimensions={0}, use_global_device_ids=true | all-gather | bytes 20736 | tf_op jit(solution)/shard_map/all_gather | solution.py:82
  24.8 24.6 %all-gather.8.cloned.1.call-done = bf16[1,512,1536]{2,1,0:T(8,128)(2,1)} async-done(((bf16[1,128,1536]{2,1,0:T(8,128)(2,1)}), bf16[1,512,1536]{2,1,0:T(8,128)(2,1)}) %all-gather.8.cloned.1.call-update) | async-done | bytes 1572880 | tf_op jit(solution)/shard_map/all_gather | solution.py:77
  59.5 24.7 %all-gather.10.cloned.1.call-done = bf16[1536,3,384]{2,0,1:T(8,128)(2,1)} async-done(((bf16[192,3,384]{2,0,1:T(8,128)(2,1)}), bf16[1536,3,384]{2,0,1:T(8,128)(2,1)}) %all-gather.10.cloned.1.call-update) | async-done | bytes 3538960 | tf_op jit(solution)/shard_map/all_gather | solution.py:81
  84.2 6.0 copy.92
  90.3 4.1 fusion.41
  96.6 2.9 collective-permute-start
  106.7 3.3 fusion.74
  110.0 2.2 copy.94
  112.1 2.2 copy.101
  118.6 37.0 %while.31 = (s32[]{:T(128)}, f32[6,512,64]{1,2,0:T(8,128)}, f32[6,512]{1,0:T(8,128)S(1)}, bf16[6,512,64]{2,1,0:T(8,128)(2,1)}, bf16[6,1024,64]{2,1,0:T(8,128)(2,...) while((s32[]{:T(128)}, f32[6,512,64]{1,2,0:T(8,128)}, ...), condition=%wide.region_8.9_spmd, body=%wide.region_5.8_spmd.sunk | while | flops 139460096 | bytes 7643265 | solution.py:163
  122.4 2.2 fusion.162
  128.6 2.3 fusion.162
  134.8 2.2 fusion.162
  140.9 2.2 fusion.162
  147.1 2.2 fusion.162
  153.2 2.2 fusion.162
  156.2 3.4 fusion.84
  159.6 4.0 fusion.128
  170.4 17.5 %collective-permute-done.4 = bf16[384,1024]{1,0:T(8,128)(2,1)S(1)} collective-permute-done((bf16[384,1024]{1,0:T(8,128)(2,1)S(1)}, bf16[384,1024]{1,0:T(8,128)(2,1)S(1)}, u32[]{:S(2)}, u32[]{:S(2)}) %collective-permute-start.4) | collective-permute-done | bytes 786464 | tf_op jit(solution)/shard_map/ppermute | solution.py:14
  191.5 93.3 %all-reduce.5.cloned.1.call-done = f32[512,1536]{1,0:T(8,128)} async-done(((f32[512,1536]{1,0:T(8,128)}), f32[512,1536]{1,0:T(8,128)}) %all-reduce.5.cloned.1.call-update) | async-done | bytes 3145744 | tf_op jit(solution)/shard_map/psum | solution.py:170
  284.8 2.8 multiply_reduce_fusion.5
  289.2 42.5 %all-gather.16.cloned.1.call-done = bf16[1536,2,1024]{2,0,1:T(8,128)(2,1)} async-done(((bf16[192,2,1024]{2,0,1:T(8,128)(2,1)}), bf16[1536,2,1024]{2,0,1:T(8,128)(2,1)}) %all-gather.16.cloned.1.call-update) | async-done | bytes 6291472 | tf_op jit(solution)/shard_map/all_gather | solution.py:85
  331.7 8.7 copy.104
  340.4 8.1 fusion.36
  348.4 22.0 %all-gather.18.cloned.1.call-done = bf16[1,512,1536]{2,1,0:T(8,128)(2,1)} async-done(((bf16[1,128,1536]{2,1,0:T(8,128)(2,1)}), bf16[1,512,1536]{2,1,0:T(8,128)(2,1)}) %all-gather.18.cloned.1.call-update) | async-done | bytes 1572880 | tf_op jit(solution)/shard_map/all_gather | solution.py:78
  370.4 7.1 fusion.52
  378.8 8.0 convolution_bitcast_fusion.2
  391.6 7.3 fusion.47
  399.2 107.8 %all-reduce.7.cloned.1.call-done = f32[512,1536]{1,0:T(8,128)} async-done(((f32[512,1536]{1,0:T(8,128)}), f32[512,1536]{1,0:T(8,128)}) %all-reduce.7.cloned.1.call-update) | async-done | bytes 3145744 | tf_op jit(solution)/shard_map/psum | solution.py:198
  507.0 3.4 multiply_reduce_fusion.1
  510.5 3.0 fusion.46
  515.3 2.2 copy.105
  519.0 97.3 %while.32 = (s32[]{:T(128)}, f32[6,512,64]{1,2,0:T(8,128)}, f32[6,1024,64]{1,2,0:T(8,128)}, f32[6,1024,64]{1,2,0:T(8,128)}, f32[6,512]{1,0:T(8,128)}, /*index=5*...) while((s32[]{:T(128)}, f32[6,512,64]{1,2,0:T(8,128)}, ...), condition=%wide.region_18.19_spmd, body=%wide.region_14.18_spmd.sunk | while | flops 342981632 | bytes 20376776 | solution.py:228
  522.1 2.1 multiply_reduce_fusion.11
  538.3 2.1 multiply_reduce_fusion.11
  554.5 2.1 multiply_reduce_fusion.11
  586.9 2.1 multiply_reduce_fusion.11
  603.1 2.1 multiply_reduce_fusion.11
  618.2 2.1 slice.88
  634.1 2.4 fusion.80
  639.4 2.7 rev.7
  643.4 4.1 reduce-window.16
  658.0 2.7 rev.8
  662.8 2.6 convolution_convert_fusion.6
  667.6 2.3 multiply_reduce_fusion.6
  674.6 2.3 convolution_bitcast_fusion.3
  678.4 3.4 multiply_reduce_fusion.2
  682.7 6.4 convolution_convert_fusion.2
  689.2 3.7 convolution_convert_fusion.5
  693.0 2.1 convolution_convert_fusion.4
  696.1 5.8 convolution_convert_fusion.1
  702.0 3.1 maximum_convert_fusion
  705.1 4.0 copy.114
  709.0 8.9 convolution_convert_fusion
  718.6 2.1 fusion.89
  722.6 41.1 %all-reduce.1 = (f32[24]{0:T(128)}, f32[1536]{0:T(1024)}, f32[1536]{0:T(1024)}, f32[2,64]{1,0:T(2,128)}) all-reduce(f32[24]{0:T(128)S(1)} %dynamic_update_slice.28, f32[1536]{0:T(1024)S(1)} %get-tuple-element.207, f32[1536]{0:T(1024)S(1)} %fusion.108, ...), channel_id=1, replica_groups=mesh['shard'=4,'ctx'=2,'tp'=4] {'shard','ctx','tp'}, use_global_device_ids=true, to_apply=%region_30.31 | all-reduce | flops 3224 | bytes 25792 | tf_op jit(solution)/shard_map/psum | solution.py:320
  764.6 8.1 reduce-scatter.26.cloned.1.call-done
  774.6 38.1 %reduce-scatter.20.cloned.1.call-done = bf16[192,384]{1,0:T(8,128)(2,1)} async-done(((bf16[1536,384]{1,0:T(8,128)(2,1)}), bf16[192,384]{1,0:T(8,128)(2,1)}) %reduce-scatter.20.cloned.1.call-update) | async-done | bytes 147472 | tf_op jit(solution)/shard_map/reduce_scatter | solution.py:303
  814.3 38.6 %reduce-scatter.22.cloned.1.call-done = bf16[192,384]{1,0:T(8,128)(2,1)} async-done(((bf16[1536,384]{1,0:T(8,128)(2,1)}), bf16[192,384]{1,0:T(8,128)(2,1)}) %reduce-scatter.22.cloned.1.call-update) | async-done | bytes 147472 | tf_op jit(solution)/shard_map/reduce_scatter | solution.py:306
  854.6 36.4 %reduce-scatter.16.cloned.1.call-done = bf16[1,128,1536]{2,1,0:T(8,128)(2,1)} async-done(((bf16[1,512,1536]{2,1,0:T(8,128)(2,1)}), bf16[1,128,1536]{2,1,0:T(8,128)(2,1)}) %reduce-scatter.16.cloned.1.call-update) | async-done | bytes 393232 | tf_op jit(solution)/shard_map/reduce_scatter | solution.py:281
  890.9 2.2 fusion.83
  893.1 48.2 %reduce-scatter.18.cloned.1.call-done = bf16[192,3,384]{2,0,1:T(8,128)(2,1)} async-done(((bf16[1536,3,384]{2,0,1:T(8,128)(2,1)}), bf16[192,3,384]{2,0,1:T(8,128)(2,1)}) %reduce-scatter.18.cloned.1.call-update) | async-done | bytes 442384 | tf_op jit(solution)/shard_map/reduce_scatter | solution.py:297
  943.4 63.0 %reduce-scatter.24.cloned.1.call-done = bf16[192,2,1024]{2,0,1:T(8,128)(2,1)} async-done(((bf16[1536,2,1024]{2,0,1:T(8,128)(2,1)}), bf16[192,2,1024]{2,0,1:T(8,128)(2,1)}) %reduce-scatter.24.cloned.1.call-update) | async-done | bytes 786448 | tf_op jit(solution)/shard_map/reduce_scatter | solution.py:309
  1006.4 3.1 copy.116
  (410 shorter events, 215.1 us)
Async XLA Ops:
  7.2 17.5 %copy-start.70 = (f32[24]{0:T(128)S(1)}, f32[24]{0:T(128)}, u32[]{:S(2)}) copy-start(f32[24]{0:T(128)} %param.24) | copy-start | bytes 292
  7.2 42.2 %all-gather.8.cloned.1.call-start = ((), (), s32[]{:S(2)}) async-start(), calls=%async_computation.9 | async-start | bytes 1966080 | tf_op jit(solution)/shard_map/all_gather | solution.py:77
  7.9 76.3 %all-gather.10.cloned.1.call-start = ((), (), s32[]{:S(2)}) async-start(), calls=%async_computation.10 | async-start | bytes 3981312 | tf_op jit(solution)/shard_map/all_gather | solution.py:81
  8.7 42.5 %copy-start.60 = (f32[1536]{0:T(1024)S(1)}, f32[1536]{0:T(1024)}, u32[]{:S(2)}) copy-start(f32[1536]{0:T(1024)} %param.29) | copy-start | bytes 18436
  8.7 146.9 %all-gather.12.cloned.1.call-start = ((), (), s32[]{:S(2)}) async-start(), calls=%async_computation.11 | async-start | bytes 1327104 | tf_op jit(solution)/shard_map/all_gather | solution.py:83
  9.4 150.2 %all-gather.14.cloned.1.call-start = ((), (), s32[]{:S(2)}) async-start(), calls=%async_computation.12 | async-start | bytes 1327104 | tf_op jit(solution)/shard_map/all_gather | solution.py:84
  10.0 274.8 %all-reduce.5.cloned.1.call-start = ((), (), s32[]{:S(2)}) async-start(), calls=%async_computation.13 | async-start | bytes 6291456 | tf_op jit(solution)/shard_map/psum | solution.py:170
  11.5 84.2 %copy-start.50 = (f32[384]{0:T(512)}, f32[384]{0:T(512)S(1)}, u32[]{:S(2)}) copy-start(f32[384]{0:T(512)S(1)} %mul.516) | copy-start | bytes 4612
  22.8 30.4 %copy-start.40 = (bf16[1536,6]{0,1:T(8,128)(2,1)}, bf16[1536,6]{0,1:T(8,128)(2,1)S(1)}, u32[]{:S(2)}) copy-start(bf16[1536,6]{0,1:T(8,128)(2,1)S(1)} %reshape.771) | copy-start | bytes 55300
  51.2 39.0 %copy-start.58 = (f32[512]{0:T(512)}, f32[512]{0:T(512)S(1)}, u32[]{:S(2)}) copy-start(f32[512]{0:T(512)S(1)} %add_rsqrt_fusion) | copy-start | bytes 6148
  53.2 5.0 copy-start.43
  55.5 2.4 collective-permute-start.1
  59.5 30.8 %copy-start.2 = (bf16[1,512,1536]{2,1,0:T(8,128)(2,1)S(1)}, bf16[1,512,1536]{2,1,0:T(8,128)(2,1)}, u32[]{:S(2)}) copy-start(bf16[1,512,1536]{2,1,0:T(8,128)(2,1)} %all-gather.8.cloned.1.call-done) | copy-start | bytes 4718596
  94.4 7.8 copy-start.4
  94.5 7.7 copy-start.9
  94.5 9.3 copy-start.6
  95.6 6.0 copy-start.38
  95.7 5.9 copy-start.36
  96.6 13.3 %collective-permute-start = (bf16[1,512,384]{1,2,0:T(8,128)(2,1)}, bf16[1,512,384]{1,2,0:T(8,128)(2,1)}, u32[]{:S(2)}, u32[]{:S(2)}) collective-permute-start(bf16[1,512,384]{1,2,0:T(8,128)(2,1)} %multiply_convert_fusion.9), channel_id=1, source_target_pairs={{0,4},{1,5},{2,6},{3,7},{8,12},{9,13},{10,14},{11,15},{16,20},{17,... | collective-permute-start | bytes 1179656 | tf_op jit(solution)/shard_map/ppermute | solution.py:25
  99.5 12.6 %collective-permute-start.2 = (bf16[1,512,384]{1,2,0:T(8,128)(2,1)}, bf16[1,512,384]{1,2,0:T(8,128)(2,1)}, u32[]{:S(2)}, u32[]{:S(2)}) collective-permute-start(bf16[1,512,384]{1,2,0:T(8,128)(2,1)} %slice_bitcast_fusion.5), channel_id=1, source_target_pairs={{0,4},{1,5},{2,6},{3,7},{8,12},{9,13},{10,14},{11,15},{16,20},{17,... | collective-permute-start | bytes 1179656 | tf_op jit(solution)/shard_map/ppermute | solution.py:25
  155.6 4.0 copy-start.10
  163.6 168.1 %all-gather.16.cloned.1.call-start = ((), (), s32[]{:S(2)}) async-start(), calls=%async_computation.14 | async-start | bytes 7077888 | tf_op jit(solution)/shard_map/all_gather | solution.py:85
  165.8 204.5 %all-gather.18.cloned.1.call-start = ((), (), s32[]{:S(2)}) async-start(), calls=%async_computation.16 | async-start | bytes 1966080 | tf_op jit(solution)/shard_map/all_gather | solution.py:78
  166.1 1.8 collective-permute-start.3
  168.2 19.6 %collective-permute-start.4 = (bf16[384,1024]{1,0:T(8,128)(2,1)S(1)}, bf16[384,1024]{1,0:T(8,128)(2,1)S(1)}, u32[]{:S(2)}, u32[]{:S(2)}) collective-permute-start(bf16[384,1024]{1,0:T(8,128)(2,1)S(1)} %maximum_select_fusion.2), channel_id=1, source_target_pairs={{0,8},{4,12},{8,0},{12,4},{16,24},{20,28},{24,16},{28,20},{1,9},{5... | collective-permute-start | bytes 2359304 | tf_op jit(solution)/shard_map/ppermute | solution.py:14
  169.7 337.3 %all-reduce.7.cloned.1.call-start = ((), (), s32[]{:S(2)}) async-start(), calls=%async_computation.17 | async-start | bytes 6291456 | tf_op jit(solution)/shard_map/psum | solution.py:198
  189.6 180.8 %collective-permute-start.5 = (bf16[768,1024]{1,0:T(8,128)(2,1)}, bf16[768,1024]{1,0:T(8,128)(2,1)}, u32[]{:S(2)}, u32[]{:S(2)}) collective-permute-start(bf16[768,1024]{1,0:T(8,128)(2,1)} %maximum_select_fusion.1), channel_id=1, source_target_pairs={{0,16},{4,20},{8,24},{12,28},{16,0},{20,4},{24,8},{28,12},{1,17},{... | collective-permute-start | bytes 4718600 | tf_op jit(solution)/shard_map/ppermute | solution.py:14
  287.7 219.3 %copy-start = (f32[512,1536]{1,0:T(8,128)}, f32[512,1536]{1,0:T(8,128)S(1)}, u32[]{:S(2)}) copy-start(f32[512,1536]{1,0:T(8,128)S(1)} %get-tuple-element.267) | copy-start | bytes 9437188
  386.9 331.7 %reduce-scatter.14.cloned.1.call-start = ((), (), s32[]{:S(2)}) async-start(), calls=%async_computation.15 | async-start | bytes 1966080 | tf_op jit(solution)/shard_map/reduce_scatter | solution.py:179
  398.9 322.0 %reduce-scatter.30.cloned.1.call-start = ((), (), s32[]{:S(2)}) async-start(), calls=%async_computation.25 | async-start | bytes 442368
  507.0 3.5 copy-start.55
  507.0 3.5 copy-start.8
  507.0 3.5 copy-start.19
  507.0 3.5 copy-start.45
  507.0 3.5 copy-start.52
  507.0 3.5 copy-start.66
  510.5 3.0 copy-start.12
  510.5 3.0 copy-start.16
  519.0 3.0 copy-start.1
  535.3 3.0 copy-start.1
  551.5 3.0 copy-start.1
  567.7 3.0 copy-start.1
  583.9 3.0 copy-start.1
  600.1 3.0 copy-start.1
  620.3 51.9 %collective-permute-start.7 = (bf16[1,512,384]{1,2,0:T(8,128)(2,1)}, bf16[1,512,384]{1,2,0:T(8,128)(2,1)}, u32[]{:S(2)}, u32[]{:S(2)}) collective-permute-start(bf16[1,512,384]{1,2,0:T(8,128)(2,1)} %bitcast.100), channel_id=1, source_target_pairs={{4,0},{5,1},{6,2},{7,3},{12,8},{13,9},{14,10},{15,11},{20,16},{21,... | collective-permute-start | bytes 1179656 | tf_op jit(solution)/shard_map/ppermute | solution.py:25
  623.6 44.0 %collective-permute-start.6 = (bf16[1,512,384]{1,2,0:T(8,128)(2,1)}, bf16[1,512,384]{1,2,0:T(8,128)(2,1)}, u32[]{:S(2)}, u32[]{:S(2)}) collective-permute-start(bf16[1,512,384]{1,2,0:T(8,128)(2,1)} %bitcast.90), channel_id=1, source_target_pairs={{4,0},{5,1},{6,2},{7,3},{12,8},{13,9},{14,10},{15,11},{20,16},{21,... | collective-permute-start | bytes 1179656 | tf_op jit(solution)/shard_map/ppermute | solution.py:25
  632.7 5.1 copy-start.24
  632.7 6.1 copy-start.35
  632.7 6.1 copy-start.39
  632.7 6.1 collective-permute-start.8
  667.1 96.6 %reduce-scatter.28.cloned.1.call-start = ((), (), s32[]{:S(2)}) async-start(), calls=%async_computation.24 | async-start | bytes 163840
  672.2 4.7 copy-start.27
  672.2 4.7 copy-start.29
  678.4 4.3 copy-start.67
  682.6 90.0 %reduce-scatter.26.cloned.1.call-start = ((), (), s32[]{:S(2)}) async-start(), calls=%async_computation.23 | async-start | bytes 3538944 | tf_op jit(solution)/shard_map/reduce_scatter | solution.py:312
  689.1 123.6 %reduce-scatter.20.cloned.1.call-start = ((), (), s32[]{:S(2)}) async-start(), calls=%async_computation.20 | async-start | bytes 1327104 | tf_op jit(solution)/shard_map/reduce_scatter | solution.py:303
  692.9 160.0 %reduce-scatter.22.cloned.1.call-start = ((), (), s32[]{:S(2)}) async-start(), calls=%async_computation.21 | async-start | bytes 1327104 | tf_op jit(solution)/shard_map/reduce_scatter | solution.py:306
  695.1 195.8 %reduce-scatter.16.cloned.1.call-start = ((), (), s32[]{:S(2)}) async-start(), calls=%async_computation.18 | async-start | bytes 1966080 | tf_op jit(solution)/shard_map/reduce_scatter | solution.py:281
  695.7 245.7 %reduce-scatter.18.cloned.1.call-start = ((), (), s32[]{:S(2)}) async-start(), calls=%async_computation.19 | async-start | bytes 3981312 | tf_op jit(solution)/shard_map/reduce_scatter | solution.py:297
  701.9 304.4 %reduce-scatter.24.cloned.1.call-start = ((), (), s32[]{:S(2)}) async-start(), calls=%async_computation.22 | async-start | bytes 7077888 | tf_op jit(solution)/shard_map/reduce_scatter | solution.py:309
  705.1 4.0 copy-start.46
  705.1 4.0 copy-start.53
  717.9 4.6 copy-start.57
  717.9 4.7 copy-start.68
  (38 other events, 67.4 us)
Sparse Core Ops, SparseCore 0:
  9.6 39.7 all-gather.7
  51.3 32.8 all-gather.9
  86.1 24.0 all-gather.11
  111.9 24.0 all-gather.13
  163.8 120.9 all-reduce.4
  287.1 44.5 all-gather.15
  333.3 37.0 all-gather.17
  387.0 119.9 all-reduce.6
  509.3 34.2 reduce-scatter.13
  667.2 35.1 reduce-scatter.29
  705.2 19.1 reduce-scatter.27
  728.0 44.5 reduce-scatter.25
  775.9 36.7 reduce-scatter.19
  816.1 36.7 reduce-scatter.21
  855.6 35.2 reduce-scatter.15
  894.3 47.0 reduce-scatter.17
  944.6 61.7 reduce-scatter.23
